TPU v7x, 32 devices: a whole 2x2x4 slice. The times are simulated.
32 devices in a mesh: groups: 2 (over y), row: 8 (over z, x), section: 2 (over core).
Axes of the slice: x: 2, y: 2, z: 4, core: 2. Of those that a mesh axis runs over, the one named last changes fastest.
Arguments:
- hidden: bfloat16 [64, 8192], P('groups', ('row', 'section')), parts along dimension 0, may hold values from -6 to 6
- norm_in_gain: float32 [8192], replicated, may hold values from 0.1 to 1.9
- zx_weight: bfloat16 [8192, 2, 8, 64], P(None, None, 'row', 'section'), may hold values from -0.0625 to 0.0625
- bc_weight: bfloat16 [8192, 2048], P(None, ('row', 'section')), may hold values from -0.0625 to 0.0625
- dt_weight: bfloat16 [8192, 8], P(None, 'row'), may hold values from -0.0625 to 0.0625
- dt_bias: float32 [8], P('row'), may hold values from -3 to -0.5
- decay_log: float32 [8], P('row'), may hold values from -0.7 to 2
- skip_gain: float32 [8], P('row'), may hold values from 0.5 to 1.5
- conv_x_weight: float32 [4, 8, 64], P(None, 'row', 'section'), may hold values from -3.6 to 3.6
- conv_x_bias: float32 [8, 64], P('row', 'section'), may hold values from -3 to 3
- conv_bc_weight: float32 [4, 2048], P(None, ('row', 'section')), may hold values from -3 to 3
- conv_bc_bias: float32 [2048], P(('row', 'section')), may hold values from -3 to 3
- conv_x_state: bfloat16 [64, 3, 8, 64], P('groups', None, 'row', 'section'), parts along dimension 0, may hold values from -6 to 6
- conv_bc_state: bfloat16 [64, 3, 2048], P('groups', None, ('row', 'section')), parts along dimension 0, may hold values from -6 to 6
- ssm_state: bfloat16 [64, 8, 64, 256], P('groups', 'row', 'section'), parts along dimension 0, may hold values from -6 to 6
- gate_norm_weight: float32 [8, 64], P('row', 'section'), may hold values from 0.1 to 1.9
- out_weight: bfloat16 [8, 64, 8192], P('row', 'section'), may hold values from -0.375 to 0.375
- norm_mid_gain: float32 [8192], replicated, may hold values from 0.1 to 1.9
- up_weight: bfloat16 [8192, 16384], P(None, ('row', 'section')), may hold values from -0.0625 to 0.0625
- down_weight: bfloat16 [16384, 8192], P(('row', 'section')), may hold values from -0.0625 to 0.0625
- valid: int32 [64], P('groups'), parts along dimension 0, may hold values 0 or 1
Outputs:
- block_out: bfloat16 [64, 8192], P('groups', ('row', 'section')), parts along dimension 0
- new_ssm_state: bfloat16 [64, 8, 64, 256], P('groups', 'row', 'section'), parts along dimension 0
- new_conv_x_state: bfloat16 [64, 3, 8, 64], P('groups', None, 'row', 'section'), parts along dimension 0
- new_conv_bc_state: bfloat16 [64, 3, 2048], P('groups', None, ('row', 'section')), parts along dimension 0
There are 2 independent parts, one for each index of `groups`. A program takes and returns all parts, laid end to end along the dimension named above; an argument that names none is the same for every part. Nothing has to cross between parts.
All inputs are finite; a program needn't handle non-finite values.
Results may differ from a plain program's by a relative error of at most 0.0075.
Values may be sent and summed in bfloat16 or wider, within the bound.
A program may use at most 128 MiB of HBM per device.

v0:
```python
import jax
import jax.numpy as jnp
from jax import lax
from jax.sharding import PartitionSpec as P

D = 8192
HEAD_DIM = 64
STATE = 256
GROUPS = 4


def mean_norm(values, gain):
    return values * lax.rsqrt(jnp.mean(values * values, axis=-1, keepdims=True) + 1e-05) * gain


def body(
    hidden,
    norm_in_gain,
    zx_weight,
    bc_weight,
    dt_weight,
    dt_bias,
    decay_log,
    skip_gain,
    conv_x_weight,
    conv_x_bias,
    conv_bc_weight,
    conv_bc_bias,
    conv_x_state,
    conv_bc_state,
    ssm_state,
    gate_norm_weight,
    out_weight,
    norm_mid_gain,
    up_weight,
    down_weight,
    valid,
):
    row_count = hidden.shape[0]
    local_p = zx_weight.shape[3]
    full_rows = lax.all_gather(hidden, ("row", "section"), axis=1, tiled=True)
    normed = mean_norm(full_rows.astype(jnp.float32), norm_in_gain).astype(jnp.bfloat16)
    gate_inner = jnp.dot(
        normed, zx_weight.reshape(D, 2 * local_p), preferred_element_type=jnp.float32
    ).reshape(row_count, 2, 1, local_p)
    gate_part = gate_inner[:, 0]
    inner_pre = gate_inner[:, 1].astype(jnp.bfloat16)
    bc_pre = jnp.dot(normed, bc_weight, preferred_element_type=jnp.float32).astype(jnp.bfloat16)
    dt_raw = jnp.dot(normed, dt_weight, preferred_element_type=jnp.float32)
    taps_x = jnp.concatenate([conv_x_state, inner_pre[:, None]], axis=1)
    inner = jax.nn.silu(
        jnp.sum(taps_x.astype(jnp.float32) * conv_x_weight[None], axis=1) + conv_x_bias
    )
    taps_bc = jnp.concatenate([conv_bc_state, bc_pre[:, None]], axis=1)
    mixed_bc = jax.nn.silu(
        jnp.sum(taps_bc.astype(jnp.float32) * conv_bc_weight[None], axis=1) + conv_bc_bias
    )
    all_bc = lax.all_gather(mixed_bc, ("row", "section"), axis=1, tiled=True)
    per_group = lax.axis_size("row") // GROUPS
    group_index = lax.axis_index("row") // per_group
    state_in = all_bc[:, : GROUPS * STATE].reshape(row_count, GROUPS, STATE)
    state_out = all_bc[:, GROUPS * STATE :].reshape(row_count, GROUPS, STATE)
    in_mine = lax.dynamic_slice_in_dim(state_in, group_index, 1, axis=1)
    out_mine = lax.dynamic_slice_in_dim(state_out, group_index, 1, axis=1)
    step_size = jax.nn.softplus(dt_raw + dt_bias[None])
    decay_rate = jnp.exp(-step_size * jnp.exp(decay_log)[None])
    previous = ssm_state.astype(jnp.float32)
    updated = (
        decay_rate[:, :, None, None] * previous
        + (step_size[:, :, None] * inner)[..., None] * in_mine[:, :, None, :]
    )
    readout = (
        jnp.einsum("rhpn,rhn->rhp", updated, out_mine, precision=lax.Precision.HIGHEST)
        + skip_gain[None, :, None] * inner
    )
    gated = readout * jax.nn.silu(gate_part)
    local_squares = jnp.sum(gated * gated, axis=(1, 2))
    group_pick = (jnp.arange(GROUPS) == group_index).astype(jnp.float32)
    group_sums = lax.psum(local_squares[:, None] * group_pick[None], ("row", "section"))
    group_size = per_group * HEAD_DIM
    group_mean = jnp.sum(group_sums * group_pick[None], axis=1) / group_size
    scaled = (gated * lax.rsqrt(group_mean + 1e-05)[:, None, None] * gate_norm_weight[None]).astype(
        jnp.bfloat16
    )
    mixer_terms = jnp.dot(
        scaled.reshape(row_count, local_p),
        out_weight.reshape(local_p, D),
        preferred_element_type=jnp.float32,
    )
    mixer_share = lax.psum_scatter(mixer_terms, ("row", "section"), scatter_dimension=1, tiled=True)
    middle = (hidden.astype(jnp.float32) + mixer_share).astype(jnp.bfloat16)
    middle_full = lax.all_gather(middle, ("row", "section"), axis=1, tiled=True)
    mlp_in = mean_norm(middle_full.astype(jnp.float32), norm_mid_gain).astype(jnp.bfloat16)
    up_values = jnp.dot(mlp_in, up_weight, preferred_element_type=jnp.float32)
    activated = jnp.square(jax.nn.relu(up_values)).astype(jnp.bfloat16)
    down_terms = jnp.dot(activated, down_weight, preferred_element_type=jnp.float32)
    down_share = lax.psum_scatter(down_terms, ("row", "section"), scatter_dimension=1, tiled=True)
    block_out = (middle.astype(jnp.float32) + down_share).astype(jnp.bfloat16)
    kept_rows = valid != 0
    new_ssm_state = jnp.where(kept_rows[:, None, None, None], updated, previous).astype(
        jnp.bfloat16
    )
    new_conv_x_state = jnp.where(kept_rows[:, None, None, None], taps_x[:, 1:], conv_x_state)
    new_conv_bc_state = jnp.where(kept_rows[:, None, None], taps_bc[:, 1:], conv_bc_state)
    return (block_out, new_ssm_state, new_conv_x_state, new_conv_bc_state)


def solution(mesh):
    return jax.shard_map(
        body,
        mesh=mesh,
        in_specs=(
            P("groups", ("row", "section")),
            P(),
            P(None, None, "row", "section"),
            P(None, ("row", "section")),
            P(None, "row"),
            P("row"),
            P("row"),
            P("row"),
            P(None, "row", "section"),
            P("row", "section"),
            P(None, ("row", "section")),
            P(("row", "section")),
            P("groups", None, "row", "section"),
            P("groups", None, ("row", "section")),
            P("groups", "row", "section", None),
            P("row", "section"),
            P("row", "section", None),
            P(),
            P(None, ("row", "section")),
            P(("row", "section"), None),
            P("groups"),
        ),
        out_specs=(
            P("groups", ("row", "section")),
            P("groups", "row", "section", None),
            P("groups", None, "row", "section"),
            P("groups", None, ("row", "section")),
        ),
        check_vma=False,
    )
```

profile of v0, /device:TPU:0, one launch (start us, length us, event | category | flops | bytes accessed | tf_op | source)
XLA Modules:
  0.0 251.6 jit_solution(10273601416538449090)
XLA Ops:
  7.3 24.9 %all_gather.9 = bf16[32,8192]{1,0:T(8,128)(2,1)S(1)} all-gather(bf16[32,512]{1,0:T(8,128)(2,1)} %param.21), channel_id=1, replica_groups=mesh['groups'=2,'row'=8,'section'=2] {'row','section'}, dimensions={1}, use_global_device_ids=true | all-gather | bytes 557056 | tf_op jit(solution)/shard_map/all_gather | solution.py:41
  32.2 0.2 fusion.4
  32.4 1.7 convolution_bitcast_fusion
  34.3 0.8 multiply_reduce_fusion.1
  35.8 1.2 fusion.2
  37.0 0.8 multiply_reduce_fusion
  37.8 0.7 divide_multiply_fusion
  38.4 18.1 %all_gather.10 = f32[32,2048]{1,0:T(8,128)S(1)} all-gather(f32[32,128]{1,0:T(8,128)S(1)} %divide_multiply_fusion), channel_id=1, replica_groups=mesh['groups'=2,'row'=8,'section'=2] {'row','section'}, dimensions={1}, use_global_device_ids=true | all-gather | bytes 278528 | tf_op jit(solution)/shard_map/all_gather | solution.py:58
  58.1 1.1 multiply_exponential_fusion
  59.2 0.8 broadcast_multiply_fusion
  60.1 2.3 fusion.13
  62.4 0.8 multiply_reduce_fusion.2
  63.3 31.1 %psum.7 = f32[32,4]{0,1:T(4,128)S(1)} all-reduce(f32[32,4]{0,1:T(4,128)S(1)} %broadcast_multiply_fusion.1), channel_id=1, replica_groups=mesh['groups'=2,'row'=8,'section'=2] {'row','section'}, use_global_device_ids=true, to_apply=%region_4.5 | all-reduce | flops 128 | bytes 1024 | tf_op jit(solution)/shard_map/psum | solution.py:79
  94.5 2.5 fusion.19
  97.0 54.8 %reduce-scatter.3.cloned.1.call-done = f32[32,512]{1,0:T(8,128)} async-done(((f32[32,8192]{1,0:T(8,128)}), f32[32,512]{1,0:T(8,128)}) %reduce-scatter.3.cloned.1.call-update) | async-done | bytes 65552 | tf_op jit(solution)/shard_map/reduce_scatter | solution.py:90
  151.8 0.8 add_convert_fusion.1
  152.6 20.8 %all_gather.11 = bf16[32,8192]{1,0:T(8,128)(2,1)S(1)} all-gather(bf16[32,512]{1,0:T(8,128)(2,1)S(1)} %add_convert_fusion.1), channel_id=1, replica_groups=mesh['groups'=2,'row'=8,'section'=2] {'row','section'}, dimensions={1}, use_global_device_ids=true | all-gather | bytes 557056 | tf_op jit(solution)/shard_map/all_gather | solution.py:92
  173.5 0.2 fusion.9
  173.7 14.8 %fusion.16 = f32[32,8192]{1,0:T(8,128)} fusion(bf16[1024,8192]{1,0:T(8,128)(2,1)} %param.40, bf16[8192,1024]{1,0:T(8,128)(2,1)} %param.39, bf16[32,8192]{1,0:T(8,128)(2,1)S(1)} %all_gather.11, f32[8192]{0:T(1024)} %param.38, f32[32]{0:T(128)S(1)} %add_rsqrt_fusion), kind=kOutput, calls=%fused_computation.25 | convolution fusion | flops 1074888704 | bytes 35160192 | tf_op jit(solution)/shard_map/dot_general | solution.py:96
  188.6 0.7 fusion.35
  189.2 0.7 fusion.33
  189.9 1.2 fusion.8
  191.1 52.2 %reduce-scatter.5.cloned.1.call-done = f32[32,512]{1,0:T(8,128)} async-done(((f32[32,8192]{1,0:T(8,128)}), f32[32,512]{1,0:T(8,128)}) %reduce-scatter.5.cloned.1.call-update) | async-done | bytes 65552 | tf_op jit(solution)/shard_map/reduce_scatter | solution.py:97
  243.3 1.5 add_convert_fusion
  (31 shorter events, 0.8 us)
Async XLA Ops:
  7.2 28.6 %copy-start = (bf16[8192,128]{1,0:T(8,128)(2,1)S(1)}, bf16[8192,128]{1,0:T(8,128)(2,1)}, u32[]{:S(2)}) copy-start(bf16[8192,128]{1,0:T(8,128)(2,1)} %param.24) | copy-start | bytes 6291460
  7.2 144.6 %reduce-scatter.3.cloned.1.call-start = ((), (), s32[]{:S(2)}) async-start(), calls=%async_computation.2 | async-start | bytes 1114112 | tf_op jit(solution)/shard_map/reduce_scatter | solution.py:90
  96.9 146.4 %reduce-scatter.5.cloned.1.call-start = ((), (), s32[]{:S(2)}) async-start(), calls=%async_computation.3 | async-start | bytes 1114112 | tf_op jit(solution)/shard_map/reduce_scatter | solution.py:97
  173.7 14.8 %copy-start.4 = (s32[32]{0:T(128)S(1)}, s32[32]{0:T(128)}, u32[]{:S(2)}) copy-start(s32[32]{0:T(128)} %param.41) | copy-start | bytes 388
  173.7 14.8 %copy-start.2 = (bf16[32,3,1,32]{3,0,2,1:T(8,128)(2,1)S(1)}, bf16[32,3,1,32]{3,0,2,1:T(8,128)(2,1)}, u32[]{:S(2)}) copy-start(bf16[32,3,1,32]{3,0,2,1:T(8,128)(2,1)} %param.33) | copy-start | bytes 18436
  173.7 15.5 %copy-start.3 = (bf16[32,3,128]{2,0,1:T(8,128)(2,1)S(1)}, bf16[32,3,128]{2,0,1:T(8,128)(2,1)}, u32[]{:S(2)}) copy-start(bf16[32,3,128]{2,0,1:T(8,128)(2,1)} %param.34) | copy-start | bytes 73732
  173.7 16.2 %copy-start.1 = (bf16[32,1,32,256]{3,2,1,0:T(8,128)(2,1)S(1)}, bf16[32,1,32,256]{3,2,1,0:T(8,128)(2,1)}, u32[]{:S(2)}) copy-start(bf16[32,1,32,256]{3,2,1,0:T(8,128)(2,1)} %param.35) | copy-start | bytes 1572868
Sparse Core Ops, SparseCore 0:
  97.1 54.6 reduce-scatter.2
  188.6 54.6 reduce-scatter.4
where the time goes:
time: 252 us
  waiting for transfers between devices  107 us (42%)
  blocking collectives  95 us (38%)
  matrix products  23.5 us (9%)
  between operations  16.2 us (6%)
  other arithmetic  9.25 us (4%)
    reduce_scatter x1, waiting for transfers between devices, body(): lax.psum_scatter(mixer_terms, ('row', 'section'), scatter_dimension=1, ti...  54.8 us
    reduce_scatter x1, waiting for transfers between devices, body(): lax.psum_scatter(down_terms, ('row', 'section'), scatter_dimension=1, til...  52.2 us
    psum x1, blocking collectives, body(): lax.psum(local_squares[:, None] * group_pick[None], ('row', 'section'))  31.1 us
    all_gather x1, blocking collectives, body(): full_rows = lax.all_gather(hidden, ('row', 'section'), axis=1, tiled=True)  24.9 us
    all_gather x1, blocking collectives, body(): middle_full = lax.all_gather(middle, ('row', 'section'), axis=1, tiled=True)  20.8 us
    all_gather x1, blocking collectives, body(): all_bc = lax.all_gather(mixed_bc, ('row', 'section'), axis=1, tiled=True)  18.1 us
    dot_general x1, matrix products, body(): jnp.dot(activated, down_weight, preferred_element_type=jnp.float32)  14.8 us
  transfers between devices with their start and end apart: 2, of which 2 were waited for; matrix products, arithmetic and copies ran while one was open for 1% of the time, Pallas kernels for 0%

commit v1 on v0

--- a/solution.py
+++ b/solution.py
@@ -76,7 +76,8 @@
     gated = readout * jax.nn.silu(gate_part)
     local_squares = jnp.sum(gated * gated, axis=(1, 2))
     group_pick = (jnp.arange(GROUPS) == group_index).astype(jnp.float32)
-    group_sums = lax.psum(local_squares[:, None] * group_pick[None], ("row", "section"))
+    name_slot = lambda panel: jnp.sum(jax.lax.all_gather(panel, ("row", "section")), 0)
+    group_sums = name_slot(local_squares[:, None] * group_pick[None])
     group_size = per_group * HEAD_DIM
     group_mean = jnp.sum(group_sums * group_pick[None], axis=1) / group_size
     scaled = (gated * lax.rsqrt(group_mean + 1e-05)[:, None, None] * gate_norm_weight[None]).astype(

time: 252 us -> 240 us (0.952)
  blocking collectives: 95 us -> 82.8 us
    psum x1 -> x0, blocking collectives: 31.1 us -> none  [body(): lax.psum(local_squares[:, None] * group_pick[None], ('row', 'section'))]
    all_gather x0 -> x1, blocking collectives: none -> 18.8 us  [body(): jax.lax.all_gather(panel, ('row', 'section'))]
where the time goes in v1:
time: 240 us; the launch traced here: 239 us
  waiting for transfers between devices  107 us (45%)
  blocking collectives  82.8 us (34%)
  matrix products  23.5 us (10%)
  between operations  16.2 us (7%)
  other arithmetic  9.28 us (4%)
    reduce_scatter x1, waiting for transfers between devices, body(): lax.psum_scatter(mixer_terms, ('row', 'section'), scatter_dimension=1, ti...  54.8 us
    reduce_scatter x1, waiting for transfers between devices, body(): lax.psum_scatter(down_terms, ('row', 'section'), scatter_dimension=1, til...  52.2 us
    all_gather x1, blocking collectives, body(): full_rows = lax.all_gather(hidden, ('row', 'section'), axis=1, tiled=True)  24.9 us
    all_gather x1, blocking collectives, body(): middle_full = lax.all_gather(middle, ('row', 'section'), axis=1, tiled=True)  20.9 us
    all_gather x1, blocking collectives, body(): jax.lax.all_gather(panel, ('row', 'section'))  18.8 us
    all_gather x1, blocking collectives, body(): all_bc = lax.all_gather(mixed_bc, ('row', 'section'), axis=1, tiled=True)  18.1 us
    dot_general x1, matrix products, body(): jnp.dot(activated, down_weight, preferred_element_type=jnp.float32)  14.8 us
  transfers between devices with their start and end apart: 2, of which 2 were waited for; matrix products, arithmetic and copies ran while one was open for 1% of the time, Pallas kernels for 0%

profile of v1, /device:TPU:0, one launch (start us, length us, event | category | flops | bytes accessed | tf_op | source)
XLA Modules:
  0.0 239.4 jit_solution(13127866179666446147)
XLA Ops:
  7.3 24.9 %all_gather.13 = bf16[32,8192]{1,0:T(8,128)(2,1)S(1)} all-gather(bf16[32,512]{1,0:T(8,128)(2,1)} %param.21), channel_id=1, replica_groups=mesh['groups'=2,'row'=8,'section'=2] {'row','section'}, dimensions={1}, use_global_device_ids=true | all-gather | bytes 557056 | tf_op jit(solution)/shard_map/all_gather | solution.py:41
  32.2 0.2 fusion.4
  32.4 1.7 convolution_bitcast_fusion
  34.3 0.8 multiply_reduce_fusion.1
  35.8 1.2 fusion.2
  37.0 0.8 multiply_reduce_fusion
  37.8 0.7 divide_multiply_fusion
  38.4 18.1 %all_gather.14 = f32[32,2048]{1,0:T(8,128)S(1)} all-gather(f32[32,128]{1,0:T(8,128)S(1)} %divide_multiply_fusion), channel_id=1, replica_groups=mesh['groups'=2,'row'=8,'section'=2] {'row','section'}, dimensions={1}, use_global_device_ids=true | all-gather | bytes 278528 | tf_op jit(solution)/shard_map/all_gather | solution.py:58
  58.1 1.1 multiply_exponential_fusion
  59.2 0.8 broadcast_multiply_fusion
  60.1 2.3 fusion.13
  62.4 0.8 multiply_reduce_fusion.2
  63.3 18.8 %all_gather.15 = f32[16,32,4]{1,2,0:T(4,128)S(1)} all-gather(f32[1,32,4]{1,2,0:T(4,128)S(1)} %broadcast_multiply_fusion.1), channel_id=1, replica_groups=mesh['groups'=2,'row'=8,'section'=2] {'row','section'}, dimensions={0}, use_global_device_ids=true | all-gather | bytes 8704 | tf_op jit(solution)/shard_map/all_gather | solution.py:79
  82.2 2.4 %fusion.19 = f32[32,8192]{1,0:T(8,128)} fusion(bf16[1,32,8192]{2,1,0:T(8,128)(2,1)} %param.37, f32[32,32]{0,1:T(8,128)S(1)} %get-tuple-element.5, f32[32]{0:T(128)} %bitcast.59, f32[32]{0:T(128)S(1)} %add_rsqrt_fusion.1), kind=kOutput, calls=%fused_computation.26 | convolution fusion | flops 16780288 | bytes 1577216 | tf_op jit(solution)/shard_map/dot_general | solution.py:86
  84.8 54.8 %reduce-scatter.3.cloned.1.call-done = f32[32,512]{1,0:T(8,128)} async-done(((f32[32,8192]{1,0:T(8,128)}), f32[32,512]{1,0:T(8,128)}) %reduce-scatter.3.cloned.1.call-update) | async-done | bytes 65552 | tf_op jit(solution)/shard_map/reduce_scatter | solution.py:91
  139.6 0.8 add_convert_fusion.1
  140.4 20.9 %all_gather.16 = bf16[32,8192]{1,0:T(8,128)(2,1)S(1)} all-gather(bf16[32,512]{1,0:T(8,128)(2,1)S(1)} %add_convert_fusion.1), channel_id=1, replica_groups=mesh['groups'=2,'row'=8,'section'=2] {'row','section'}, dimensions={1}, use_global_device_ids=true | all-gather | bytes 557056 | tf_op jit(solution)/shard_map/all_gather | solution.py:93
  161.3 0.2 fusion.9
  161.6 14.8 %fusion.16 = f32[32,8192]{1,0:T(8,128)} fusion(bf16[1024,8192]{1,0:T(8,128)(2,1)} %param.40, bf16[8192,1024]{1,0:T(8,128)(2,1)} %param.39, bf16[32,8192]{1,0:T(8,128)(2,1)S(1)} %all_gather.16, f32[8192]{0:T(1024)} %param.38, f32[32]{0:T(128)S(1)} %add_rsqrt_fusion), kind=kOutput, calls=%fused_computation.25 | convolution fusion | flops 1074888704 | bytes 35160192 | tf_op jit(solution)/shard_map/dot_general | solution.py:97
  176.4 0.7 fusion.35
  177.1 0.7 fusion.33
  177.8 1.2 fusion.8
  178.9 52.2 %reduce-scatter.5.cloned.1.call-done = f32[32,512]{1,0:T(8,128)} async-done(((f32[32,8192]{1,0:T(8,128)}), f32[32,512]{1,0:T(8,128)}) %reduce-scatter.5.cloned.1.call-update) | async-done | bytes 65552 | tf_op jit(solution)/shard_map/reduce_scatter | solution.py:98
  231.1 1.5 add_convert_fusion
  (32 shorter events, 0.9 us)
Async XLA Ops:
  7.2 28.6 %copy-start = (bf16[8192,128]{1,0:T(8,128)(2,1)S(1)}, bf16[8192,128]{1,0:T(8,128)(2,1)}, u32[]{:S(2)}) copy-start(bf16[8192,128]{1,0:T(8,128)(2,1)} %param.24) | copy-start | bytes 6291460
  7.2 132.4 %reduce-scatter.3.cloned.1.call-start = ((), (), s32[]{:S(2)}) async-start(), calls=%async_computation.2 | async-start | bytes 1114112 | tf_op jit(solution)/shard_map/reduce_scatter | solution.py:91
  84.7 146.4 %reduce-scatter.5.cloned.1.call-start = ((), (), s32[]{:S(2)}) async-start(), calls=%async_computation.3 | async-start | bytes 1114112 | tf_op jit(solution)/shard_map/reduce_scatter | solution.py:98
  161.5 14.8 %copy-start.4 = (s32[32]{0:T(128)S(1)}, s32[32]{0:T(128)}, u32[]{:S(2)}) copy-start(s32[32]{0:T(128)} %param.41) | copy-start | bytes 388
  161.5 14.8 %copy-start.2 = (bf16[32,3,1,32]{3,0,2,1:T(8,128)(2,1)S(1)}, bf16[32,3,1,32]{3,0,2,1:T(8,128)(2,1)}, u32[]{:S(2)}) copy-start(bf16[32,3,1,32]{3,0,2,1:T(8,128)(2,1)} %param.33) | copy-start | bytes 18436
  161.5 15.5 %copy-start.3 = (bf16[32,3,128]{2,0,1:T(8,128)(2,1)S(1)}, bf16[32,3,128]{2,0,1:T(8,128)(2,1)}, u32[]{:S(2)}) copy-start(bf16[32,3,128]{2,0,1:T(8,128)(2,1)} %param.34) | copy-start | bytes 73732
  161.5 16.2 %copy-start.1 = (bf16[32,1,32,256]{3,2,1,0:T(8,128)(2,1)S(1)}, bf16[32,1,32,256]{3,2,1,0:T(8,128)(2,1)}, u32[]{:S(2)}) copy-start(bf16[32,1,32,256]{3,2,1,0:T(8,128)(2,1)} %param.35) | copy-start | bytes 1572868
Sparse Core Ops, SparseCore 0:
  84.8 54.6 reduce-scatter.2
  176.5 54.5 reduce-scatter.4
